TPU v7x, 512 devices: a whole 4x8x8 slice. The times are simulated.
512 devices in a mesh: cons: 4 (over y_hi), ty: 8 (over x, y_lo), tx: 16 (over z, core).
Axes of the slice: x: 4, y: 8 (y_hi: 4, y_lo: 2; y = y_hi * 2 + y_lo), z: 8, core: 2. Of those that a mesh axis runs over, the one named last changes fastest.
Arguments:
- elevation: float32 [8, 2, 1152, 8192], P('cons', None, 'ty', 'tx'), may hold values from -6 to 6
- equilibrium: float32 [8, 2, 1152, 8192], P('cons', None, 'ty', 'tx'), may hold values from -5 to 5
- depth: float32 [1152, 8192], P('ty', 'tx'), may hold values from 0.1 to 1
- land_mask: int32 [1152, 8192], P('ty', 'tx'), may hold values 0 or 1
- friction_prev: float32 [1152, 8192], P('ty', 'tx'), may hold values from 0.3 to 3
Outputs:
- elevation_out: float32 [8, 2, 1152, 8192], P('cons', None, 'ty', 'tx')
- friction: float32 [1152, 8192], P('ty', 'tx')
All inputs are finite; a program needn't handle non-finite values. No bound on the sum of `land_mask` on one device may be relied on, other than what follows from the above.
Results may differ from a plain program's by a relative error of at most 0.00002.
Values sent between devices are 32-bit elements; how exact they have to be, the bound alone decides.
A program may use at most 64 MiB of HBM per device.

v0:
```python
import math
import jax
import jax.numpy as jnp
from jax import lax
from jax.sharding import PartitionSpec as P

OMEGA_TABLE = (1.0, 1.0351, 0.9582, 1.0379, 0.5181, 0.4816, 0.5164, 0.4454)
AY_SCALE = 0.5
THETA = 0.05
DRAG = 0.5
BACKGROUND = 0.01


def passed_along(value, axis, steps):
    count = lax.axis_size(axis)
    pairs = [(source, (source + steps) % count) for source in range(count)]
    return lax.ppermute(value, axis, pairs)


def passed_along_2(block, axis, distance):
    devices = range(lax.axis_size(axis))
    route = [(i - distance, i) for i in devices if i - distance in devices]
    return lax.ppermute(block, axis, route)


def latitude_factor(rows, total):
    lat = (-60.0 + 120.0 * (rows.astype(jnp.float32) + 0.5) / total) * (math.pi / 180.0)
    return 0.5 / jnp.cos(lat)


def momentum(num_re, num_im, fric, omega, face_mask):
    denom = fric * fric + omega * omega
    return (
        face_mask * (num_re * fric + num_im * omega) / denom,
        face_mask * (num_im * fric - num_re * omega) / denom,
    )


def ahead_rims(planes):
    east_col = passed_along(planes[:, :, 0], "tx", -1)
    north_row = passed_along_2(planes[:, 0, :], "ty", -1)
    return (east_col, north_row)


def forward_rims(planes):
    east_col, north_row = ahead_rims(planes)
    east_view = jnp.concatenate([planes[:, :, 1:], east_col[:, :, None]], axis=2)
    north_view = jnp.concatenate([planes[:, 1:, :], north_row[:, None, :]], axis=1)
    return (east_view, north_view)


def backward_rims(trans_u, trans_v):
    west_col = passed_along(trans_u[..., :, -1], "tx", 1)
    south_row = passed_along_2(trans_v[..., -1, :], "ty", 1)
    west_u = jnp.concatenate([west_col[..., None], trans_u[..., :, :-1]], axis=-1)
    south_v = jnp.concatenate([south_row[..., None, :], trans_v[..., :-1, :]], axis=-2)
    return (west_u, south_v)


def finish(eta, trans_u, west_u, trans_v, south_v, omega, ax_rows, maskf, depth):
    div = ax_rows * (trans_u - west_u) + AY_SCALE * (trans_v - south_v)
    res = jnp.stack([-omega * eta[:, 1] + div[:, 0], omega * eta[:, 0] + div[:, 1]], axis=1)
    eta_new = maskf * (eta - THETA * res)
    cu = 0.5 * (trans_u + west_u)
    cv = 0.5 * (trans_v + south_v)
    term = 0.5 * (
        cu[:, 0] * cu[:, 0] + cu[:, 1] * cu[:, 1] + cv[:, 0] * cv[:, 0] + cv[:, 1] * cv[:, 1]
    )
    variance_part = jnp.sum(term, axis=0) / (depth * depth)
    return (eta_new, variance_part)


def sweep_core(eta, zeta, zeta_east, zeta_north, fric, fric_east, fric_north, omega, statics):
    ax_rows, maskf, mu_face, mv_face, hu_face, hv_face, depth = statics
    grad_x = ax_rows * (zeta_east - zeta)
    grad_y = AY_SCALE * (zeta_north - zeta)
    fric_u = 0.5 * (fric + fric_east)
    fric_v = 0.5 * (fric + fric_north)
    u_re, u_im = momentum(-hu_face * grad_x[:, 0], -hu_face * grad_x[:, 1], fric_u, omega, mu_face)
    v_re, v_im = momentum(-hv_face * grad_y[:, 0], -hv_face * grad_y[:, 1], fric_v, omega, mv_face)
    trans_u = jnp.stack([u_re, u_im], axis=1)
    trans_v = jnp.stack([v_re, v_im], axis=1)
    west_u, south_v = backward_rims(trans_u, trans_v)
    return finish(eta, trans_u, west_u, trans_v, south_v, omega, ax_rows, maskf, depth)


def compute_friction(variance_local, depth):
    variance_total = lax.psum(variance_local, "cons")
    return DRAG * jnp.sqrt(variance_total + BACKGROUND) / depth


def body(elevation, equilibrium, depth, land_mask, friction_prev):
    kdev, two, rows_dev, cols_dev = elevation.shape
    first_cons = lax.axis_index("cons") * kdev
    omega = lax.dynamic_slice_in_dim(jnp.array(OMEGA_TABLE, dtype=jnp.float32), first_cons, kdev)[
        :, None, None
    ]
    rows = lax.axis_index("ty") * rows_dev + jnp.arange(rows_dev, dtype=jnp.int32)
    ax_rows = latitude_factor(rows, rows_dev * lax.axis_size("ty"))[:, None]
    maskf = land_mask.astype(jnp.float32)
    planes_count = kdev * 2
    zeta = elevation - equilibrium
    planes = jnp.concatenate(
        [
            zeta.reshape(planes_count, rows_dev, cols_dev),
            friction_prev[None],
            depth[None],
            maskf[None],
        ],
        axis=0,
    )
    east_view, north_view = forward_rims(planes)
    depth_east = east_view[planes_count + 1]
    depth_north = north_view[planes_count + 1]
    mask_east = east_view[planes_count + 2]
    mask_north = north_view[planes_count + 2]
    statics = (
        ax_rows,
        maskf,
        maskf * mask_east,
        maskf * mask_north,
        0.5 * (depth + depth_east),
        0.5 * (depth + depth_north),
        depth,
    )
    eta_one, variance_local = sweep_core(
        elevation,
        zeta,
        east_view[:planes_count].reshape(kdev, 2, rows_dev, cols_dev),
        north_view[:planes_count].reshape(kdev, 2, rows_dev, cols_dev),
        friction_prev,
        east_view[planes_count],
        north_view[planes_count],
        omega,
        statics,
    )
    friction = compute_friction(variance_local, depth)
    zeta_two = eta_one - equilibrium
    planes_two = jnp.concatenate(
        [zeta_two.reshape(planes_count, rows_dev, cols_dev), friction[None]], axis=0
    )
    east_two, north_two = forward_rims(planes_two)
    eta_two, unused = sweep_core(
        eta_one,
        zeta_two,
        east_two[:planes_count].reshape(kdev, 2, rows_dev, cols_dev),
        north_two[:planes_count].reshape(kdev, 2, rows_dev, cols_dev),
        friction,
        east_two[planes_count],
        north_two[planes_count],
        omega,
        statics,
    )
    return (eta_two, friction)


def solution(mesh):
    return jax.shard_map(
        body,
        mesh=mesh,
        in_specs=(
            P("cons", None, "ty", "tx"),
            P("cons", None, "ty", "tx"),
            P("ty", "tx"),
            P("ty", "tx"),
            P("ty", "tx"),
        ),
        out_specs=(P("cons", None, "ty", "tx"), P("ty", "tx")),
        check_vma=False,
    )
```

profile of v0, /device:TPU:1, one launch (start us, length us, event | category | flops | bytes accessed | tf_op | source)
XLA Modules:
  0.0 136.4 jit_solution(13368709324180972753)
XLA Ops:
  7.2 1.7 %fusion.62 = (f32[144,512]{1,0:T(8,128)}, f32[1,144,512]{2,1,0:T(8,128)S(1)}) fusion(s32[144,512]{1,0:T(8,128)} %param.9), kind=kLoop, calls=%fused_computation.150 | loop fusion | flops 73728 | bytes 884736 | tf_op jit(solution)/shard_map/convert_element_type | solution.py:100
  8.9 1.9 %sub.52 = f32[2,2,144,512]{3,2,1,0:T(8,128)S(1)} subtract(f32[2,2,144,512]{3,2,1,0:T(8,128)} %param.6, f32[2,2,144,512]{3,2,1,0:T(8,128)} %param.7) | non-fusion elementwise | flops 294912 | bytes 3538944 | tf_op jit(solution)/shard_map/sub | solution.py:102
  10.9 1.3 collective-permute-start.2
  12.4 0.9 slice_reduce_fusion
  13.3 6.9 %collective-permute-start = (f32[7,144]{1,0:T(8,128)}, f32[7,144]{1,0:T(8,128)}, u32[]{:S(2)}, u32[]{:S(2)}) collective-permute-start(f32[7,144]{1,0:T(8,128)} %slice_reduce_fusion), channel_id=1, source_target_pairs={{0,15},{1,0},{2,1},{3,2},{4,3},{5,4},{6,5},{7,6},{8,7},{9,8},{10,9... | collective-permute-start | bytes 12104 | tf_op jit(solution)/shard_map/ppermute | solution.py:17
  20.2 1.3 dynamic-slice_negate_fusion
  22.1 1.8 %slice.206 = f32[7,143,512]{2,1,0:T(8,128)} slice(f32[7,144,512]{2,1,0:T(8,128)S(1)} %pad_maximum_fusion), slice={[0:7], [1:144], [0:512]} | slice | bytes 4100096 | tf_op jit(solution)/shard_map/slice | solution.py:48
  23.9 1.9 %slice.196 = f32[7,144,511]{2,1,0:T(8,128)} slice(f32[7,144,512]{2,1,0:T(8,128)S(1)} %pad_maximum_fusion), slice={[0:7], [0:144], [1:512]} | slice | bytes 4120704 | tf_op jit(solution)/shard_map/slice | solution.py:47
  25.8 1.9 %copy.28 = f32[7,144,1]{2,1,0:T(8,128)} copy(f32[7,144,1]{1,0,2:T(8,128)} %bitcast.4) | data formatting | bytes 8064 | tf_op jit(solution)/shard_map/broadcast_in_dim | solution.py:47
  27.6 1.6 %fusion.14 = f32[4,144,512]{2,1,0:T(8,128)S(1)} fusion(f32[7,144,511]{2,1,0:T(8,128)} %slice.196, f32[7,144,1]{2,1,0:T(8,128)} %copy.28), kind=kLoop, calls=%fused_computation.49 | loop fusion | flops 294912 | bytes 3244032 | tf_op jit(solution)/shard_map/concatenate | solution.py:47
  30.0 1.5 %fusion.60 = (f32[144,512]{1,0:T(8,128)S(1)}, f32[144,512]{1,0:T(8,128)S(1)}, f32[144,512]{1,0:T(8,128)S(1)}, f32[144,512]{1,0:T(8,128)S(1)}, f32[144,512]{1,0:T...) fusion(f32[144,512]{1,0:T(8,128)} %param.10, ...), kind=kLoop, calls=%fused_computation.149 | loop fusion | flops 1548288 | bytes 7372800 | tf_op jit(solution)/shard_map/mul | solution.py:32
  32.8 0.8 add_divide_fusion.7
  33.9 1.1 fusion.12
  35.1 4.3 %collective-permute-start.3 = (f32[2,2,512]{2,1,0:T(2,128)S(1)}, f32[2,2,512]{2,1,0:T(2,128)S(1)}, u32[]{:S(2)}, u32[]{:S(2)}) collective-permute-start(f32[2,2,512]{2,1,0:T(2,128)S(1)} %bitcast.102), channel_id=1, source_target_pairs={{0,16},{16,32},{32,48},{48,64},{64,80},{80,96},{96,112},{1,17},{17... | collective-permute-start | bytes 24584 | tf_op jit(solution)/shard_map/ppermute | solution.py:23
  39.4 1.1 fusion.8
  40.7 3.4 %add_multiply_fusion.1 = (f32[2,2,144,512]{3,2,1,0:T(8,128)S(1)}, f32[2,2,144,512]{3,2,1,0:T(8,128)}, f32[2,2,144,512]{3,2,1,0:T(8,128)S(1)}) fusion(f32[2,1,144,512]{3,2,1,0:T(8,128)S(1)} %get-tuple-element.22, f32[2,1,144,512]{3,2,1,0:T(8,128)S(1)} %get-tuple-element.21, f32[2,2,144,511]{3,2,1,0:T(8,128)} %fusion.12, f32[2,2,144,1]{3,2,1,0:T(8,128)S(1)} %copy.29, ...), kind=kLoop, calls=%fused_computation.61 | loop fusion | flops 3833856 | bytes 8258112 | tf_op jit(solution)/shard_map/mul | solution.py:64
  46.2 0.9 copy-done.7
  47.2 1.5 %fusion.56 = (f32[2,2,144,512]{3,2,1,0:T(8,128)S(1)}, f32[2,2,144,512]{3,2,1,0:T(8,128)}) fusion(f32[2,2,144,512]{3,2,1,0:T(8,128)S(1)} %copy-done.7, f32[2,2,144,512]{3,2,1,0:T(8,128)S(1)} %copy-done.4, f32[2,1,144,512]{3,2,1,0:T(8,128)S(1)} %get-tuple-element.28, f32[2,1,144,512]{3,2,1,0:T(8,128)S(1)} %get-tuple-element.27, f32[144,512]{1,0:T(8,128)S(1)} %copy-done.10), kind=kLoop, calls=%fused_computation.147 | loop fusion | flops 1474560 | bytes 6193152 | tf_op jit(solution)/shard_map/sub | solution.py:138
  48.7 52.7 %all-reduce.2.cloned.1.call-done = f32[144,512]{1,0:T(8,128)} async-done(((f32[144,512]{1,0:T(8,128)}), f32[144,512]{1,0:T(8,128)}) %all-reduce.2.cloned.1.call-update) | async-done | bytes 294928 | tf_op jit(solution)/shard_map/psum | solution.py:88
  101.4 1.1 multiply_divide_fusion
  102.7 1.6 %fusion.1 = f32[5,144,511]{2,1,0:T(8,128)} fusion(f32[4,144,512]{2,1,0:T(8,128)S(1)} %bitcast.82, f32[1,144,512]{2,1,0:T(8,128)S(1)} %bitcast.88), kind=kLoop, calls=%fused_computation.32 | loop fusion | flops 367920 | bytes 2946240 | tf_op jit(solution)/shard_map/concatenate | solution.py:139
  104.6 2.7 %collective-permute-start.4 = (f32[5,144]{1,0:T(8,128)S(1)}, f32[5,144]{1,0:T(8,128)S(1)}, u32[]{:S(2)}, u32[]{:S(2)}) collective-permute-start(f32[5,144]{1,0:T(8,128)S(1)} %fusion.25), channel_id=1, source_target_pairs={{0,15},{1,0},{2,1},{3,2},{4,3},{5,4},{6,5},{7,6},{8,7},{9,8},{10,9... | collective-permute-start | bytes 8648 | tf_op jit(solution)/shard_map/ppermute | solution.py:17
  107.3 1.3 collective-permute-start.6
  108.6 1.3 collective-permute-done.4
  110.0 1.5 %fusion.3 = f32[4,144,512]{2,1,0:T(8,128)S(1)} fusion(f32[5,144,511]{2,1,0:T(8,128)} %fusion.1, f32[5,144,1]{2,1,0:T(8,128)S(1)} %copy.31), kind=kLoop, calls=%fused_computation.38 | loop fusion | flops 294912 | bytes 2654208 | tf_op jit(solution)/shard_map/concatenate | solution.py:47
  113.3 0.8 add_divide_fusion.3
  114.6 2.5 %collective-permute-start.5 = (f32[2,2,144]{2,1,0:T(2,128)S(1)}, f32[2,2,144]{2,1,0:T(2,128)S(1)}, u32[]{:S(2)}, u32[]{:S(2)}) collective-permute-start(f32[2,2,144]{2,1,0:T(2,128)S(1)} %fusion.27), channel_id=1, source_target_pairs={{0,1},{1,2},{2,3},{3,4},{4,5},{5,6},{6,7},{7,8},{8,9},{9,10},{10,1... | collective-permute-start | bytes 6920 | tf_op jit(solution)/shard_map/ppermute | solution.py:17
  117.0 4.2 %collective-permute-start.7 = (f32[2,2,512]{2,1,0:T(2,128)S(1)}, f32[2,2,512]{2,1,0:T(2,128)}, u32[]{:S(2)}, u32[]{:S(2)}) collective-permute-start(f32[2,2,512]{2,1,0:T(2,128)S(1)} %bitcast.103), channel_id=1, source_target_pairs={{0,16},{16,32},{32,48},{48,64},{64,80},{80,96},{96,112},{1,17},{17... | collective-permute-start | bytes 24584 | tf_op jit(solution)/shard_map/ppermute | solution.py:23
  121.2 1.1 fusion.4
  122.9 1.5 %copy.32 = f32[2,2,144,1]{3,2,1,0:T(8,128)} copy(f32[2,2,144,1]{2,1,0,3:T(2,128)} %bitcast.106) | data formatting | bytes 4608 | tf_op jit(solution)/shard_map/broadcast_in_dim | solution.py:55
  125.1 2.1 %fusion.7 = f32[2,2,144,512]{3,2,1,0:T(8,128)S(1)} fusion(f32[2,1,144,512]{3,2,1,0:T(8,128)S(1)} %get-tuple-element.43, f32[2,1,144,512]{3,2,1,0:T(8,128)S(1)} %get-tuple-element.44, f32[2,1,144,512]{3,2,1,0:T(8,128)S(1)} %get-tuple-element.18, f32[2,1,144,512]{3,2,1,0:T(8,128)S(1)} %get-tuple-element.17, f32[2,2,144,511]{3,2,1,0:T(8,128)S(1)} %fusion.9, ...), kind=kLoop, calls=%fused_computation.42 | loop fusion | flops 2654208 | bytes 5898816 | tf_op jit(solution)/shard_map/add | solution.py:61
  128.2 1.3 fusion.18
  (91 shorter events, 10.6 us)
Async XLA Ops:
  7.2 94.2 %all-reduce.2.cloned.1.call-start = ((), (), s32[]{:S(2)}) async-start(), calls=%async_computation | async-start | bytes 589824 | tf_op jit(solution)/shard_map/psum | solution.py:88
  8.9 1.9 %copy-start.6 = (f32[144,512]{1,0:T(8,128)S(1)}, f32[144,512]{1,0:T(8,128)}, u32[]{:S(2)}) copy-start(f32[144,512]{1,0:T(8,128)} %param.8) | copy-start | bytes 884740
  8.9 1.9 %copy-start.9 = (f32[144,512]{1,0:T(8,128)S(1)}, f32[144,512]{1,0:T(8,128)}, u32[]{:S(2)}) copy-start(f32[144,512]{1,0:T(8,128)} %param.10) | copy-start | bytes 884740
  10.9 18.4 %collective-permute-start.2 = (f32[7,512]{1,0:T(8,128)S(1)}, f32[7,512]{1,0:T(8,128)}, u32[]{:S(2)}, u32[]{:S(2)}) collective-permute-start(f32[7,512]{1,0:T(8,128)S(1)} %bitcast.99), channel_id=1, source_target_pairs={{16,0},{32,16},{48,32},{64,48},{80,64},{96,80},{112,96},{17,1},{33... | collective-permute-start | bytes 43016 | tf_op jit(solution)/shard_map/ppermute | solution.py:23
  13.3 12.4 %collective-permute-start = (f32[7,144]{1,0:T(8,128)}, f32[7,144]{1,0:T(8,128)}, u32[]{:S(2)}, u32[]{:S(2)}) collective-permute-start(f32[7,144]{1,0:T(8,128)} %slice_reduce_fusion), channel_id=1, source_target_pairs={{0,15},{1,0},{2,1},{3,2},{4,3},{5,4},{6,5},{7,6},{8,7},{9,8},{10,9... | collective-permute-start | bytes 12104 | tf_op jit(solution)/shard_map/ppermute | solution.py:17
  25.8 4.2 %copy-start.1 = (f32[7,144,511]{2,1,0:T(8,128)S(1)}, f32[7,144,511]{2,1,0:T(8,128)}, u32[]{:S(2)}) copy-start(f32[7,144,511]{2,1,0:T(8,128)} %slice.196) | copy-start | bytes 6181060
  27.6 2.4 %copy-start = (f32[7,143,512]{2,1,0:T(8,128)S(1)}, f32[7,143,512]{2,1,0:T(8,128)}, u32[]{:S(2)}) copy-start(f32[7,143,512]{2,1,0:T(8,128)} %slice.206) | copy-start | bytes 6150148
  31.5 1.1 copy-start.12
  31.5 1.1 copy-start.14
  31.5 1.1 copy-start.16
  31.6 1.1 copy-start.18
  31.6 0.6 copy-start.20
  35.1 5.4 %collective-permute-start.1 = (f32[2,2,144]{2,1,0:T(2,128)S(1)}, f32[2,2,144]{2,1,0:T(2,128)S(1)}, u32[]{:S(2)}, u32[]{:S(2)}) collective-permute-start(f32[2,2,144]{2,1,0:T(2,128)S(1)} %fusion.29), channel_id=1, source_target_pairs={{0,1},{1,2},{2,3},{3,4},{4,5},{5,6},{6,7},{7,8},{8,9},{9,10},{10,1... | collective-permute-start | bytes 6920 | tf_op jit(solution)/shard_map/ppermute | solution.py:17
  35.1 5.6 %collective-permute-start.3 = (f32[2,2,512]{2,1,0:T(2,128)S(1)}, f32[2,2,512]{2,1,0:T(2,128)S(1)}, u32[]{:S(2)}, u32[]{:S(2)}) collective-permute-start(f32[2,2,512]{2,1,0:T(2,128)S(1)} %bitcast.102), channel_id=1, source_target_pairs={{0,16},{16,32},{32,48},{48,64},{64,80},{80,96},{96,112},{1,17},{17... | collective-permute-start | bytes 24584 | tf_op jit(solution)/shard_map/ppermute | solution.py:23
  44.1 1.3 copy-start.8
  44.4 1.5 %copy-start.4 = (f32[2,2,144,512]{3,2,1,0:T(8,128)S(1)}, f32[2,2,144,512]{3,2,1,0:T(8,128)}, u32[]{:S(2)}) copy-start(f32[2,2,144,512]{3,2,1,0:T(8,128)} %param.6) | copy-start | bytes 3538948
  44.4 1.5 %copy-start.22 = (f32[2]{0:T(128)S(1)}, f32[2]{0:T(128)}, u32[]{:S(2)}) copy-start(f32[2]{0:T(128)} %get-tuple-element.47) | copy-start | bytes 28
  45.9 1.3 copy-start.7
  45.9 1.3 copy-start.10
  102.5 9.3 %copy-start.3 = (f32[144,512]{1,0:T(8,128)}, f32[144,512]{1,0:T(8,128)S(1)}, u32[]{:S(2)}) copy-start(f32[144,512]{1,0:T(8,128)S(1)} %multiply_divide_fusion) | copy-start | bytes 884740
  104.6 5.3 %collective-permute-start.4 = (f32[5,144]{1,0:T(8,128)S(1)}, f32[5,144]{1,0:T(8,128)S(1)}, u32[]{:S(2)}, u32[]{:S(2)}) collective-permute-start(f32[5,144]{1,0:T(8,128)S(1)} %fusion.25), channel_id=1, source_target_pairs={{0,15},{1,0},{2,1},{3,2},{4,3},{5,4},{6,5},{7,6},{8,7},{9,8},{10,9... | collective-permute-start | bytes 8648 | tf_op jit(solution)/shard_map/ppermute | solution.py:17
  107.3 4.5 %collective-permute-start.6 = (f32[5,512]{1,0:T(8,128)S(1)}, f32[5,512]{1,0:T(8,128)S(1)}, u32[]{:S(2)}, u32[]{:S(2)}) collective-permute-start(f32[5,512]{1,0:T(8,128)S(1)} %bitcast.100), channel_id=1, source_target_pairs={{16,0},{32,16},{48,32},{64,48},{80,64},{96,80},{112,96},{17,1},{33... | collective-permute-start | bytes 30728 | tf_op jit(solution)/shard_map/ppermute | solution.py:23
  110.0 1.7 %copy-start.2 = (f32[5,144,511]{2,1,0:T(8,128)S(1)}, f32[5,144,511]{2,1,0:T(8,128)}, u32[]{:S(2)}) copy-start(f32[5,144,511]{2,1,0:T(8,128)} %fusion.1) | copy-start | bytes 4415044
  112.1 1.0 copy-start.13
  112.1 1.0 copy-start.15
  112.1 1.1 copy-start.17
  112.1 1.2 copy-start.19
  114.6 7.7 %collective-permute-start.5 = (f32[2,2,144]{2,1,0:T(2,128)S(1)}, f32[2,2,144]{2,1,0:T(2,128)S(1)}, u32[]{:S(2)}, u32[]{:S(2)}) collective-permute-start(f32[2,2,144]{2,1,0:T(2,128)S(1)} %fusion.27), channel_id=1, source_target_pairs={{0,1},{1,2},{2,3},{3,4},{4,5},{5,6},{6,7},{7,8},{8,9},{9,10},{10,1... | collective-permute-start | bytes 6920 | tf_op jit(solution)/shard_map/ppermute | solution.py:17
  117.0 7.4 %collective-permute-start.7 = (f32[2,2,512]{2,1,0:T(2,128)S(1)}, f32[2,2,512]{2,1,0:T(2,128)}, u32[]{:S(2)}, u32[]{:S(2)}) collective-permute-start(f32[2,2,512]{2,1,0:T(2,128)S(1)} %bitcast.103), channel_id=1, source_target_pairs={{0,16},{16,32},{32,48},{48,64},{64,80},{80,96},{96,112},{1,17},{17... | collective-permute-start | bytes 24584 | tf_op jit(solution)/shard_map/ppermute | solution.py:23
  125.1 2.1 %copy-start.5 = (f32[2,2,144,512]{3,2,1,0:T(8,128)S(1)}, f32[2,2,144,512]{3,2,1,0:T(8,128)}, u32[]{:S(2)}) copy-start(f32[2,2,144,512]{3,2,1,0:T(8,128)} %get-tuple-element.7) | copy-start | bytes 3538948
  125.1 2.1 %copy-start.23 = (f32[2]{0:T(128)S(1)}, f32[2]{0:T(128)}, u32[]{:S(2)}) copy-start(f32[2]{0:T(128)} %get-tuple-element.47) | copy-start | bytes 28
  127.2 1.0 copy-start.11
  (3 other events, 1.8 us)
Sparse Core Ops, SparseCore 0:
  45.3 56.0 all-reduce.1
where the time goes:
time: 137 us; the launch traced here: 136 us
  waiting for transfers between devices  54.2 us (40%)
  other arithmetic  30.5 us (22%)
  starting transfers between devices  23 us (17%)
  between operations  14.5 us (11%)
  local copies, waits for them, and re-layouts  14.2 us (10%)
    psum x1, waiting for transfers between devices, compute_friction(): variance_total = lax.psum(variance_local, 'cons')  52.7 us
    ppermute x4, starting transfers between devices, passed_along(): return lax.ppermute(value, axis, pairs)  12 us
    ppermute x4, starting transfers between devices, passed_along_2(): return lax.ppermute(block, axis, route)  11 us
    unnamed x56, local copies, waits for them, and re-layouts  4.38 us
    mul x1, other arithmetic, finish(): cu = 0.5 * (trans_u + west_u)  3.39 us
    concatenate x2, other arithmetic, forward_rims(): jnp.concatenate([planes[:, :, 1:], east_col[:, :, None]], axis=2)  3.17 us
  transfers between devices with their start and end apart: 9, of which 3 were waited for; matrix products, arithmetic and copies ran while one was open for 13% of the time, Pallas kernels for 0%

commit v1 on v0

--- a/solution.py
+++ b/solution.py
@@ -9,6 +9,12 @@
 THETA = 0.05
 DRAG = 0.5
 BACKGROUND = 0.01
+
+
+def summed_here(x, name):
+    parts = lax.all_gather(x, name, axis=0, tiled=False)
+    acc = parts.sum(axis=0)
+    return acc
 
 
 def passed_along(value, axis, steps):
@@ -85,7 +91,7 @@
 
 
 def compute_friction(variance_local, depth):
-    variance_total = lax.psum(variance_local, "cons")
+    variance_total = summed_here(variance_local, "cons")
     return DRAG * jnp.sqrt(variance_total + BACKGROUND) / depth
 
 

time: 137 us -> 121 us (0.88)
  waiting for transfers between devices: 54.2 us -> 39.2 us
  starting transfers between devices: 23 us -> 21.3 us
    psum x1 -> x0, waiting for transfers between devices: 52.7 us -> none  [compute_friction(): variance_total = lax.psum(variance_local, 'cons')]
    all_gather x0 -> x1, waiting for transfers between devices: none -> 37.8 us  [summed_here(): parts = lax.all_gather(x, name, axis=0, tiled=False)]
    ppermute x4, starting transfers between devices: 12 us -> 9.95 us  [passed_along(): return lax.ppermute(value, axis, pairs)]
    reduce_sum x0 -> x1, other arithmetic: none -> 1.4 us  [summed_here(): acc = parts.sum(axis=0)]
  transfers between devices with their start and end apart: 9 -> 9, of which waited for: 3 -> 3; matrix products, arithmetic and copies ran while one was open for 13% -> 15% of each run, Pallas kernels for 0% -> 0%
where the time goes in v1:
time: 121 us; the launch traced here: 120 us
  waiting for transfers between devices  39.2 us (32%)
  other arithmetic  30.9 us (26%)
  starting transfers between devices  21.3 us (18%)
  between operations  14.5 us (12%)
  local copies, waits for them, and re-layouts  14.1 us (12%)
    all_gather x1, waiting for transfers between devices, summed_here(): parts = lax.all_gather(x, name, axis=0, tiled=False)  37.8 us
    ppermute x4, starting transfers between devices, passed_along_2(): return lax.ppermute(block, axis, route)  11.3 us
    ppermute x4, starting transfers between devices, passed_along(): return lax.ppermute(value, axis, pairs)  9.95 us
    unnamed x56, local copies, waits for them, and re-layouts  4.37 us
    mul x1, other arithmetic, finish(): cu = 0.5 * (trans_u + west_u)  3.39 us
    concatenate x2, other arithmetic, forward_rims(): jnp.concatenate([planes[:, :, 1:], east_col[:, :, None]], axis=2)  3.17 us
  transfers between devices with their start and end apart: 9, of which 3 were waited for; matrix products, arithmetic and copies ran while one was open for 15% of the time, Pallas kernels for 0%

profile of v1, /device:TPU:1, one launch (start us, length us, event | category | flops | bytes accessed | tf_op | source)
XLA Modules:
  0.0 120.1 jit_solution(137248660780644397)
XLA Ops:
  7.2 1.7 %fusion.62 = (f32[144,512]{1,0:T(8,128)}, f32[1,144,512]{2,1,0:T(8,128)S(1)}) fusion(s32[144,512]{1,0:T(8,128)} %param.9), kind=kLoop, calls=%fused_computation.150 | loop fusion | flops 73728 | bytes 884736 | tf_op jit(solution)/shard_map/convert_element_type | solution.py:106
  8.9 1.9 %sub.52 = f32[2,2,144,512]{3,2,1,0:T(8,128)S(1)} subtract(f32[2,2,144,512]{3,2,1,0:T(8,128)} %param.6, f32[2,2,144,512]{3,2,1,0:T(8,128)} %param.7) | non-fusion elementwise | flops 294912 | bytes 3538944 | tf_op jit(solution)/shard_map/sub | solution.py:108
  10.9 1.3 %collective-permute-start.2 = (f32[7,512]{1,0:T(8,128)S(1)}, f32[7,512]{1,0:T(8,128)}, u32[]{:S(2)}, u32[]{:S(2)}) collective-permute-start(f32[7,512]{1,0:T(8,128)S(1)} %bitcast.101), channel_id=1, source_target_pairs={{16,0},{32,16},{48,32},{64,48},{80,64},{96,80},{112,96},{17,1},{33... | collective-permute-start | bytes 43016 | tf_op jit(solution)/shard_map/ppermute | solution.py:29
  12.4 0.9 slice_reduce_fusion
  13.3 6.9 %collective-permute-start = (f32[7,144]{1,0:T(8,128)}, f32[7,144]{1,0:T(8,128)}, u32[]{:S(2)}, u32[]{:S(2)}) collective-permute-start(f32[7,144]{1,0:T(8,128)} %slice_reduce_fusion), channel_id=1, source_target_pairs={{0,15},{1,0},{2,1},{3,2},{4,3},{5,4},{6,5},{7,6},{8,7},{9,8},{10,9... | collective-permute-start | bytes 12104 | tf_op jit(solution)/shard_map/ppermute | solution.py:23
  20.2 1.3 %dynamic-slice_negate_fusion = (f32[2]{0:T(128)}, f32[2]{0:T(128)}, f32[2]{0:T(128)}) fusion(f32[8]{0:T(128)} %constant.41.clone, s32[]{:T(128)S(6)} %select_n.3), kind=kLoop, calls=%fused_computation.144 | loop fusion | flops 4 | bytes 36 | tf_op jit(solution)/shard_map/neg | solution.py:68
  22.1 1.8 %slice.206 = f32[7,143,512]{2,1,0:T(8,128)} slice(f32[7,144,512]{2,1,0:T(8,128)S(1)} %pad_maximum_fusion), slice={[0:7], [1:144], [0:512]} | slice | bytes 4100096 | tf_op jit(solution)/shard_map/slice | solution.py:54
  23.9 1.9 %slice.196 = f32[7,144,511]{2,1,0:T(8,128)} slice(f32[7,144,512]{2,1,0:T(8,128)S(1)} %pad_maximum_fusion), slice={[0:7], [0:144], [1:512]} | slice | bytes 4120704 | tf_op jit(solution)/shard_map/slice | solution.py:53
  25.8 1.9 %copy.28 = f32[7,144,1]{2,1,0:T(8,128)} copy(f32[7,144,1]{1,0,2:T(8,128)} %bitcast.4) | data formatting | bytes 8064 | tf_op jit(solution)/shard_map/broadcast_in_dim | solution.py:53
  27.6 1.6 %fusion.14 = f32[4,144,512]{2,1,0:T(8,128)S(1)} fusion(f32[7,144,511]{2,1,0:T(8,128)} %slice.196, f32[7,144,1]{2,1,0:T(8,128)} %copy.28), kind=kLoop, calls=%fused_computation.49 | loop fusion | flops 294912 | bytes 3244032 | tf_op jit(solution)/shard_map/concatenate | solution.py:53
  30.0 1.5 %fusion.60 = (f32[144,512]{1,0:T(8,128)S(1)}, f32[144,512]{1,0:T(8,128)S(1)}, f32[144,512]{1,0:T(8,128)S(1)}, f32[144,512]{1,0:T(8,128)S(1)}, f32[144,512]{1,0:T...) fusion(f32[144,512]{1,0:T(8,128)} %param.10, ...), kind=kLoop, calls=%fused_computation.149 | loop fusion | flops 1548288 | bytes 7372800 | tf_op jit(solution)/shard_map/mul | solution.py:38
  32.8 0.8 add_divide_fusion.7
  33.9 1.1 fusion.12
  35.1 4.3 %collective-permute-start.3 = (f32[2,2,512]{2,1,0:T(2,128)S(1)}, f32[2,2,512]{2,1,0:T(2,128)S(1)}, u32[]{:S(2)}, u32[]{:S(2)}) collective-permute-start(f32[2,2,512]{2,1,0:T(2,128)S(1)} %bitcast.104), channel_id=1, source_target_pairs={{0,16},{16,32},{32,48},{48,64},{64,80},{80,96},{96,112},{1,17},{17... | collective-permute-start | bytes 24584 | tf_op jit(solution)/shard_map/ppermute | solution.py:29
  39.4 1.1 fusion.8
  40.7 3.4 %add_multiply_fusion.1 = (f32[2,2,144,512]{3,2,1,0:T(8,128)S(1)}, f32[2,2,144,512]{3,2,1,0:T(8,128)}, f32[2,2,144,512]{3,2,1,0:T(8,128)S(1)}) fusion(f32[2,1,144,512]{3,2,1,0:T(8,128)S(1)} %get-tuple-element.22, f32[2,1,144,512]{3,2,1,0:T(8,128)S(1)} %get-tuple-element.21, f32[2,2,144,511]{3,2,1,0:T(8,128)} %fusion.12, f32[2,2,144,1]{3,2,1,0:T(8,128)S(1)} %copy.29, ...), kind=kLoop, calls=%fused_computation.61 | loop fusion | flops 3833856 | bytes 8258112 | tf_op jit(solution)/shard_map/mul | solution.py:70
  46.2 0.9 copy-done.7
  47.2 1.5 %fusion.56 = (f32[2,2,144,512]{3,2,1,0:T(8,128)S(1)}, f32[2,2,144,512]{3,2,1,0:T(8,128)}) fusion(f32[2,2,144,512]{3,2,1,0:T(8,128)S(1)} %copy-done.7, f32[2,2,144,512]{3,2,1,0:T(8,128)S(1)} %copy-done.4, f32[2,1,144,512]{3,2,1,0:T(8,128)S(1)} %get-tuple-element.28, f32[2,1,144,512]{3,2,1,0:T(8,128)S(1)} %get-tuple-element.27, f32[144,512]{1,0:T(8,128)S(1)} %copy-done.10), kind=kLoop, calls=%fused_computation.147 | loop fusion | flops 1474560 | bytes 6193152 | tf_op jit(solution)/shard_map/sub | solution.py:144
  48.7 37.8 %all-gather.3.cloned.1.call-done = f32[576,512]{1,0:T(8,128)} async-done(((f32[144,512]{1,0:T(8,128)}), f32[576,512]{1,0:T(8,128)}) %all-gather.3.cloned.1.call-update) | async-done | bytes 1179664 | tf_op jit(solution)/shard_map/all_gather | solution.py:15
  86.5 1.4 %reduce_sum.19 = f32[144,512]{1,0:T(8,128)S(1)} reduce(f32[4,144,512]{2,1,0:T(8,128)} %bitcast.100, f32[]{:T(128)} %constant.14.clone.1), dimensions={0}, to_apply=%region_1.0 | reduce | flops 221184 | bytes 1474564 | tf_op jit(solution)/shard_map/reduce_sum | solution.py:16
  88.3 1.6 %fusion.1 = f32[5,144,511]{2,1,0:T(8,128)} fusion(f32[4,144,512]{2,1,0:T(8,128)S(1)} %bitcast.83, f32[1,144,512]{2,1,0:T(8,128)S(1)} %bitcast.89), kind=kLoop, calls=%fused_computation.32 | loop fusion | flops 367920 | bytes 2946240 | tf_op jit(solution)/shard_map/concatenate | solution.py:145
  90.1 0.9 collective-permute-start.4
  91.0 1.3 %collective-permute-start.6 = (f32[5,512]{1,0:T(8,128)S(1)}, f32[5,512]{1,0:T(8,128)S(1)}, u32[]{:S(2)}, u32[]{:S(2)}) collective-permute-start(f32[5,512]{1,0:T(8,128)S(1)} %bitcast.102), channel_id=1, source_target_pairs={{16,0},{32,16},{48,32},{64,48},{80,64},{96,80},{112,96},{17,1},{33... | collective-permute-start | bytes 30728 | tf_op jit(solution)/shard_map/ppermute | solution.py:29
  92.3 1.0 collective-permute-done.4
  93.5 1.5 %fusion.3 = f32[4,144,512]{2,1,0:T(8,128)S(1)} fusion(f32[5,144,511]{2,1,0:T(8,128)} %fusion.1, f32[5,144,1]{2,1,0:T(8,128)S(1)} %copy.31), kind=kLoop, calls=%fused_computation.38 | loop fusion | flops 294912 | bytes 2654208 | tf_op jit(solution)/shard_map/concatenate | solution.py:53
  97.0 0.8 add_divide_fusion.3
  98.3 2.2 %collective-permute-start.5 = (f32[2,2,144]{2,1,0:T(2,128)S(1)}, f32[2,2,144]{2,1,0:T(2,128)S(1)}, u32[]{:S(2)}, u32[]{:S(2)}) collective-permute-start(f32[2,2,144]{2,1,0:T(2,128)S(1)} %fusion.27), channel_id=1, source_target_pairs={{0,1},{1,2},{2,3},{3,4},{4,5},{5,6},{6,7},{7,8},{8,9},{9,10},{10,1... | collective-permute-start | bytes 6920 | tf_op jit(solution)/shard_map/ppermute | solution.py:23
  100.5 4.4 %collective-permute-start.7 = (f32[2,2,512]{2,1,0:T(2,128)S(1)}, f32[2,2,512]{2,1,0:T(2,128)}, u32[]{:S(2)}, u32[]{:S(2)}) collective-permute-start(f32[2,2,512]{2,1,0:T(2,128)S(1)} %bitcast.105), channel_id=1, source_target_pairs={{0,16},{16,32},{32,48},{48,64},{64,80},{80,96},{96,112},{1,17},{17... | collective-permute-start | bytes 24584 | tf_op jit(solution)/shard_map/ppermute | solution.py:29
  104.9 1.1 fusion.4
  106.6 1.5 %copy.32 = f32[2,2,144,1]{3,2,1,0:T(8,128)} copy(f32[2,2,144,1]{2,1,0,3:T(2,128)} %bitcast.108) | data formatting | bytes 4608 | tf_op jit(solution)/shard_map/broadcast_in_dim | solution.py:61
  108.9 2.1 %fusion.7 = f32[2,2,144,512]{3,2,1,0:T(8,128)S(1)} fusion(f32[2,1,144,512]{3,2,1,0:T(8,128)S(1)} %get-tuple-element.43, f32[2,1,144,512]{3,2,1,0:T(8,128)S(1)} %get-tuple-element.44, f32[2,1,144,512]{3,2,1,0:T(8,128)S(1)} %get-tuple-element.18, f32[2,1,144,512]{3,2,1,0:T(8,128)S(1)} %get-tuple-element.17, f32[2,2,144,511]{3,2,1,0:T(8,128)S(1)} %fusion.9, ...), kind=kLoop, calls=%fused_computation.42 | loop fusion | flops 2654208 | bytes 5898816 | tf_op jit(solution)/shard_map/add | solution.py:67
  111.9 1.3 %fusion.18 = f32[2,2,144,512]{3,2,1,0:T(8,128)} fusion(f32[2,2,144,512]{3,2,1,0:T(8,128)S(1)} %copy-done.5, f32[2,1,144,512]{3,2,1,0:T(8,128)S(1)} %get-tuple-element.26, f32[2,1,144,512]{3,2,1,0:T(8,128)S(1)} %get-tuple-element.25, f32[144,512]{1,0:T(8,128)S(1)} %copy-done.11), kind=kLoop, calls=%fused_computation.57 | loop fusion | flops 1179648 | bytes 3833856 | tf_op jit(solution)/shard_map/mul | solution.py:69
  (92 shorter events, 10.9 us)
Async XLA Ops:
  7.2 79.3 %all-gather.3.cloned.1.call-start = ((), (), s32[]{:S(2)}) async-start(), calls=%async_computation | async-start | bytes 1474560 | tf_op jit(solution)/shard_map/all_gather | solution.py:15
  8.9 1.9 %copy-start.6 = (f32[144,512]{1,0:T(8,128)S(1)}, f32[144,512]{1,0:T(8,128)}, u32[]{:S(2)}) copy-start(f32[144,512]{1,0:T(8,128)} %param.8) | copy-start | bytes 884740
  8.9 1.9 %copy-start.9 = (f32[144,512]{1,0:T(8,128)S(1)}, f32[144,512]{1,0:T(8,128)}, u32[]{:S(2)}) copy-start(f32[144,512]{1,0:T(8,128)} %param.10) | copy-start | bytes 884740
  10.9 18.4 %collective-permute-start.2 = (f32[7,512]{1,0:T(8,128)S(1)}, f32[7,512]{1,0:T(8,128)}, u32[]{:S(2)}, u32[]{:S(2)}) collective-permute-start(f32[7,512]{1,0:T(8,128)S(1)} %bitcast.101), channel_id=1, source_target_pairs={{16,0},{32,16},{48,32},{64,48},{80,64},{96,80},{112,96},{17,1},{33... | collective-permute-start | bytes 43016 | tf_op jit(solution)/shard_map/ppermute | solution.py:29
  13.3 12.4 %collective-permute-start = (f32[7,144]{1,0:T(8,128)}, f32[7,144]{1,0:T(8,128)}, u32[]{:S(2)}, u32[]{:S(2)}) collective-permute-start(f32[7,144]{1,0:T(8,128)} %slice_reduce_fusion), channel_id=1, source_target_pairs={{0,15},{1,0},{2,1},{3,2},{4,3},{5,4},{6,5},{7,6},{8,7},{9,8},{10,9... | collective-permute-start | bytes 12104 | tf_op jit(solution)/shard_map/ppermute | solution.py:23
  25.8 4.2 %copy-start.1 = (f32[7,144,511]{2,1,0:T(8,128)S(1)}, f32[7,144,511]{2,1,0:T(8,128)}, u32[]{:S(2)}) copy-start(f32[7,144,511]{2,1,0:T(8,128)} %slice.196) | copy-start | bytes 6181060
  27.6 2.4 %copy-start = (f32[7,143,512]{2,1,0:T(8,128)S(1)}, f32[7,143,512]{2,1,0:T(8,128)}, u32[]{:S(2)}) copy-start(f32[7,143,512]{2,1,0:T(8,128)} %slice.206) | copy-start | bytes 6150148
  31.5 1.1 copy-start.12
  31.5 1.1 copy-start.14
  31.5 1.1 copy-start.16
  31.6 1.1 copy-start.18
  31.6 0.6 copy-start.20
  35.1 5.4 %collective-permute-start.1 = (f32[2,2,144]{2,1,0:T(2,128)S(1)}, f32[2,2,144]{2,1,0:T(2,128)S(1)}, u32[]{:S(2)}, u32[]{:S(2)}) collective-permute-start(f32[2,2,144]{2,1,0:T(2,128)S(1)} %fusion.29), channel_id=1, source_target_pairs={{0,1},{1,2},{2,3},{3,4},{4,5},{5,6},{6,7},{7,8},{8,9},{9,10},{10,1... | collective-permute-start | bytes 6920 | tf_op jit(solution)/shard_map/ppermute | solution.py:23
  35.1 5.6 %collective-permute-start.3 = (f32[2,2,512]{2,1,0:T(2,128)S(1)}, f32[2,2,512]{2,1,0:T(2,128)S(1)}, u32[]{:S(2)}, u32[]{:S(2)}) collective-permute-start(f32[2,2,512]{2,1,0:T(2,128)S(1)} %bitcast.104), channel_id=1, source_target_pairs={{0,16},{16,32},{32,48},{48,64},{64,80},{80,96},{96,112},{1,17},{17... | collective-permute-start | bytes 24584 | tf_op jit(solution)/shard_map/ppermute | solution.py:29
  44.1 1.3 %copy-start.8 = (f32[2,2,144,512]{3,2,1,0:T(8,128)S(1)}, f32[2,2,144,512]{3,2,1,0:T(8,128)}, u32[]{:S(2)}) copy-start(f32[2,2,144,512]{3,2,1,0:T(8,128)} %get-tuple-element.13) | copy-start | bytes 3538948
  44.4 1.5 %copy-start.4 = (f32[2,2,144,512]{3,2,1,0:T(8,128)S(1)}, f32[2,2,144,512]{3,2,1,0:T(8,128)}, u32[]{:S(2)}) copy-start(f32[2,2,144,512]{3,2,1,0:T(8,128)} %param.6) | copy-start | bytes 3538948
  44.4 1.5 %copy-start.22 = (f32[2]{0:T(128)S(1)}, f32[2]{0:T(128)}, u32[]{:S(2)}) copy-start(f32[2]{0:T(128)} %get-tuple-element.47) | copy-start | bytes 28
  45.9 1.3 %copy-start.7 = (f32[2,2,144,512]{3,2,1,0:T(8,128)S(1)}, f32[2,2,144,512]{3,2,1,0:T(8,128)}, u32[]{:S(2)}) copy-start(f32[2,2,144,512]{3,2,1,0:T(8,128)} %param.7) | copy-start | bytes 3538948
  45.9 1.3 %copy-start.10 = (f32[144,512]{1,0:T(8,128)S(1)}, f32[144,512]{1,0:T(8,128)}, u32[]{:S(2)}) copy-start(f32[144,512]{1,0:T(8,128)} %get-tuple-element.41) | copy-start | bytes 884740
  88.0 7.5 %copy-start.3 = (f32[144,512]{1,0:T(8,128)}, f32[144,512]{1,0:T(8,128)S(1)}, u32[]{:S(2)}) copy-start(f32[144,512]{1,0:T(8,128)S(1)} %multiply_divide_fusion) | copy-start | bytes 884740
  90.1 3.2 %collective-permute-start.4 = (f32[5,144]{1,0:T(8,128)S(1)}, f32[5,144]{1,0:T(8,128)S(1)}, u32[]{:S(2)}, u32[]{:S(2)}) collective-permute-start(f32[5,144]{1,0:T(8,128)S(1)} %fusion.25), channel_id=1, source_target_pairs={{0,15},{1,0},{2,1},{3,2},{4,3},{5,4},{6,5},{7,6},{8,7},{9,8},{10,9... | collective-permute-start | bytes 8648 | tf_op jit(solution)/shard_map/ppermute | solution.py:23
  91.0 4.5 %collective-permute-start.6 = (f32[5,512]{1,0:T(8,128)S(1)}, f32[5,512]{1,0:T(8,128)S(1)}, u32[]{:S(2)}, u32[]{:S(2)}) collective-permute-start(f32[5,512]{1,0:T(8,128)S(1)} %bitcast.102), channel_id=1, source_target_pairs={{16,0},{32,16},{48,32},{64,48},{80,64},{96,80},{112,96},{17,1},{33... | collective-permute-start | bytes 30728 | tf_op jit(solution)/shard_map/ppermute | solution.py:29
  93.5 2.0 %copy-start.2 = (f32[5,144,511]{2,1,0:T(8,128)S(1)}, f32[5,144,511]{2,1,0:T(8,128)}, u32[]{:S(2)}) copy-start(f32[5,144,511]{2,1,0:T(8,128)} %fusion.1) | copy-start | bytes 4415044
  95.8 1.0 copy-start.13
  95.8 1.0 copy-start.15
  95.8 1.1 copy-start.17
  95.8 1.2 %copy-start.19 = (f32[144,512]{1,0:T(8,128)S(1)}, f32[144,512]{1,0:T(8,128)}, u32[]{:S(2)}) copy-start(f32[144,512]{1,0:T(8,128)} %copy-done.18) | copy-start | bytes 884740
  98.3 7.7 %collective-permute-start.5 = (f32[2,2,144]{2,1,0:T(2,128)S(1)}, f32[2,2,144]{2,1,0:T(2,128)S(1)}, u32[]{:S(2)}, u32[]{:S(2)}) collective-permute-start(f32[2,2,144]{2,1,0:T(2,128)S(1)} %fusion.27), channel_id=1, source_target_pairs={{0,1},{1,2},{2,3},{3,4},{4,5},{5,6},{6,7},{7,8},{8,9},{9,10},{10,1... | collective-permute-start | bytes 6920 | tf_op jit(solution)/shard_map/ppermute | solution.py:23
  100.5 7.7 %collective-permute-start.7 = (f32[2,2,512]{2,1,0:T(2,128)S(1)}, f32[2,2,512]{2,1,0:T(2,128)}, u32[]{:S(2)}, u32[]{:S(2)}) collective-permute-start(f32[2,2,512]{2,1,0:T(2,128)S(1)} %bitcast.105), channel_id=1, source_target_pairs={{0,16},{16,32},{32,48},{48,64},{64,80},{80,96},{96,112},{1,17},{17... | collective-permute-start | bytes 24584 | tf_op jit(solution)/shard_map/ppermute | solution.py:29
  108.9 2.1 %copy-start.5 = (f32[2,2,144,512]{3,2,1,0:T(8,128)S(1)}, f32[2,2,144,512]{3,2,1,0:T(8,128)}, u32[]{:S(2)}) copy-start(f32[2,2,144,512]{3,2,1,0:T(8,128)} %get-tuple-element.7) | copy-start | bytes 3538948
  108.9 2.1 %copy-start.23 = (f32[2]{0:T(128)S(1)}, f32[2]{0:T(128)}, u32[]{:S(2)}) copy-start(f32[2]{0:T(128)} %get-tuple-element.47) | copy-start | bytes 28
  111.0 1.0 copy-start.11
  (3 other events, 1.8 us)
Sparse Core Ops, SparseCore 0:
  45.3 41.1 all-gather.2
